TPU v7x, 256 devices: a whole 4x4x8 slice. The times are simulated.
256 devices in a mesh: lat: 4 (over y_lo, core), lon: 16 (over y_hi, z), ch: 4 (over x).
Axes of the slice: x: 4, y: 4 (y_hi: 2, y_lo: 2; y = y_hi * 2 + y_lo), z: 8, core: 2. Of those that a mesh axis runs over, the one named last changes fastest.
Arguments:
- grid_field: bfloat16 [1440, 4, 49152], P('lon', 'ch', 'lat'), may hold values from -6 to 6
- first_weight: bfloat16 [4, 2, 96, 96], P('ch'), may hold values from -0.4375 to 0.4375
- first_bias: float32 [4, 2, 96], P('ch'), may hold values from -3 to 3
- second_weight: bfloat16 [4, 2, 96, 96], P('ch'), may hold values from -0.4375 to 0.4375
- second_bias: float32 [4, 2, 96], P('ch'), may hold values from -3 to 3
Outputs:
- mixed: bfloat16 [1440, 4, 49152], P('lon', 'ch', 'lat')
All inputs are finite; a program needn't handle non-finite values.
Results may differ from a plain program's by a relative error of at most 0.0073.
Values may be sent and summed in bfloat16 or wider, within the bound.
No kernel may reach another device: no remote copies, remote signals or barrier semaphores. Data moves between devices by JAX's collectives and lax.ppermute only.
A program may use at most 128 MiB of HBM per device.

v0:
```python
import math
import jax
import jax.numpy as jnp
from jax import lax
from jax.sharding import PartitionSpec as P

shrink_level = 0.01


def phase_tables(length):
    indices = jnp.arange(length, dtype=jnp.int32)
    product = indices[:, None] * indices[None, :] % length
    angles = product.astype(jnp.float32) * (2.0 * math.pi / length)
    return (jnp.cos(angles), jnp.sin(angles))


def lon_tables(length):
    cosine_tab, sine_tab = phase_tables(length)
    kept_modes = length // 2
    factor = 1.0 / math.sqrt(length)
    forward = jnp.concatenate([cosine_tab[:kept_modes], -sine_tab[:kept_modes]], axis=0) * factor
    weights = jnp.where(jnp.arange(kept_modes) == 0, 1.0, 2.0).astype(jnp.float32)
    inverse = (
        jnp.concatenate(
            [cosine_tab[:, :kept_modes] * weights, -sine_tab[:, :kept_modes] * weights], axis=1
        )
        * factor
    )
    return (forward.astype(jnp.bfloat16), inverse.astype(jnp.bfloat16))


def lat_tables(length):
    cosine_tab, sine_tab = phase_tables(length)
    factor = 1.0 / math.sqrt(length)
    forward = (
        jnp.stack(
            [jnp.stack([cosine_tab, sine_tab], axis=1), jnp.stack([-sine_tab, cosine_tab], axis=1)],
            axis=0,
        )
        * factor
    )
    inverse = (
        jnp.stack(
            [jnp.stack([cosine_tab, -sine_tab], axis=1), jnp.stack([sine_tab, cosine_tab], axis=1)],
            axis=0,
        )
        * factor
    )
    return (forward.astype(jnp.bfloat16), inverse.astype(jnp.bfloat16))


def complex_blocks(weight):
    real_part, imag_part = (weight[:, 0], weight[:, 1])
    return jnp.stack(
        [jnp.stack([real_part, imag_part], axis=2), jnp.stack([-imag_part, real_part], axis=2)],
        axis=1,
    )


def block_mixing(mode_data, first_weight, first_bias, second_weight, second_bias):
    shape = mode_data.shape
    blocks_here = first_weight.shape[0]
    block_width = first_weight.shape[2]
    split_data = mode_data.reshape(shape[0], shape[1], shape[2], blocks_here, block_width)
    hidden = jnp.einsum(
        "rkqbc,brcsd->skqbd",
        split_data,
        complex_blocks(first_weight),
        preferred_element_type=jnp.float32,
    )
    hidden = jax.nn.relu(hidden + jnp.moveaxis(first_bias, 1, 0)[:, None, None, :, :]).astype(
        jnp.bfloat16
    )
    output = jnp.einsum(
        "rkqbc,brcsd->skqbd",
        hidden,
        complex_blocks(second_weight),
        preferred_element_type=jnp.float32,
    )
    output = output + jnp.moveaxis(second_bias, 1, 0)[:, None, None, :, :]
    shrunk = jnp.sign(output) * jnp.maximum(jnp.abs(output) - shrink_level, 0.0)
    return shrunk.astype(jnp.bfloat16).reshape(shape)


def lat_apply(data, table):
    columns = lax.all_to_all(data, "lat", split_axis=3, concat_axis=2, tiled=True)
    result = jnp.einsum(
        "sqrh,rkhc->skqc", table, columns, preferred_element_type=jnp.float32
    ).astype(jnp.bfloat16)
    return lax.all_to_all(result, "lat", split_axis=2, concat_axis=3, tiled=True)


def per_device(grid_field, first_weight, first_bias, second_weight, second_bias):
    lon_devices = lax.axis_size("lon")
    lat_devices = lax.axis_size("lat")
    block_width = first_weight.shape[2]
    local_lon, blocks_here, merged = grid_field.shape
    local_lat = merged // block_width
    local_chan = blocks_here * block_width
    lon_size = local_lon * lon_devices
    lat_size = local_lat * lat_devices
    kept_modes = lon_size // 2
    lon_forward, lon_inverse = lon_tables(lon_size)
    lat_forward, lat_inverse = lat_tables(lat_size)
    reordered = grid_field.reshape(local_lon, blocks_here, local_lat, block_width).transpose(
        0, 2, 1, 3
    )
    flattened = reordered.reshape(local_lon, local_lat * local_chan)
    gathered = lax.all_to_all(flattened, "lon", split_axis=1, concat_axis=0, tiled=True)
    spectra = jnp.dot(lon_forward, gathered, preferred_element_type=jnp.float32).astype(
        jnp.bfloat16
    )
    spectra = spectra.reshape(2, kept_modes, gathered.shape[1])
    spectra = lax.all_to_all(spectra, "lon", split_axis=1, concat_axis=2, tiled=True)
    spectra = spectra.reshape(2, spectra.shape[1], local_lat, local_chan)
    mode_data = lat_apply(spectra, lat_forward)
    shrunk = block_mixing(mode_data, first_weight, first_bias, second_weight, second_bias)
    returned = lat_apply(shrunk, lat_inverse)
    returned = returned.reshape(2, returned.shape[1], local_lat * local_chan)
    returned = lax.all_to_all(returned, "lon", split_axis=2, concat_axis=1, tiled=True)
    columns = returned.reshape(2 * kept_modes, returned.shape[2])
    grid_out = jnp.dot(lon_inverse, columns, preferred_element_type=jnp.float32) + gathered.astype(
        jnp.float32
    )
    grid_out = lax.all_to_all(
        grid_out.astype(jnp.bfloat16), "lon", split_axis=0, concat_axis=1, tiled=True
    )
    grid_out = grid_out.reshape(local_lon, local_lat, blocks_here, block_width).transpose(
        0, 2, 1, 3
    )
    return grid_out.reshape(grid_field.shape)


def solution(mesh):
    in_specs = (
        P("lon", "ch", "lat"),
        P("ch", None, None, None),
        P("ch", None, None),
        P("ch", None, None, None),
        P("ch", None, None),
    )
    out_specs = P("lon", "ch", "lat")
    return jax.shard_map(
        per_device, mesh=mesh, in_specs=in_specs, out_specs=out_specs, check_vma=False
    )
```

profile of v0, /device:TPU:38, one launch (start us, length us, event | category | flops | bytes accessed | tf_op | source)
XLA Modules:
  0.0 631.3 jit_solution(6902518026747214721)
XLA Ops:
  4.5 11.2 %all-to-all-start = ((bf16[90,16,768]{2,0,1:T(8,128)(2,1)}), bf16[90,16,768]{2,0,1:T(8,128)(2,1)S(1)}, u32[]{:S(2)}, u32[]{:S(2)}) async-start(bf16[90,16,768]{2,0,1:T(8,128)(2,1)} %copy.81), calls=%async_computation | async-start | bytes 4718592 | tf_op jit(solution)/shard_map/all_to_all | solution.py:109
  15.7 36.9 %fusion.6 = (f32[1440,1440]{1,0:T(8,128)S(1)}, f32[1440,1440]{1,0:T(8,128)S(1)}) fusion(), kind=kLoop, calls=%fused_computation.10 | loop fusion | flops 18662400 | bytes 16588800 | tf_op jit(solution)/shard_map/sin | solution.py:14
  62.4 8.7 %all-to-all-done = bf16[90,16,768]{2,0,1:T(8,128)(2,1)S(1)} async-done(((bf16[90,16,768]{2,0,1:T(8,128)(2,1)}), bf16[90,16,768]{2,0,1:T(8,128)(2,1)S(1)}, u32[]{:S(2)}, u32[]{:S(2)}) %all-to-all-start) | async-done | bytes 2211872 | tf_op jit(solution)/shard_map/all_to_all | solution.py:109
  73.2 7.8 %fusion.20 = bf16[1440,768]{1,0:T(8,128)(2,1)S(1)} fusion(bf16[1440,768]{1,0:T(8,128)(2,1)} %all_to_all.99, f32[720,1440]{1,0:T(8,128)} %slice_negate_fusion, f32[720,1440]{1,0:T(8,128)} %slice.34), kind=kOutput, calls=%fused_computation.33 | convolution fusion | flops 3192376320 | bytes 12718080 | tf_op jit(solution)/shard_map/dot_general | solution.py:110
  82.8 61.5 %all_to_all.131 = bf16[2,720,768]{2,0,1:T(2,128)(2,1)S(1)} all-to-all(bf16[2,720,768]{2,0,1:T(2,128)(2,1)S(1)} %copy.82), channel_id=1, replica_groups=mesh['lat'=4,'lon'=16,'ch'=4] {'lon'}, dimensions={1} | all-to-all | bytes 4423680 | tf_op jit(solution)/shard_map/all_to_all | solution.py:114
  171.1 14.9 %all-to-all-done.2 = bf16[2,45,128,96]{2,0,1,3:T(2,128)(2,1)S(1)} async-done(((bf16[2,45,128,96]{2,0,1,3:T(2,128)(2,1)}), bf16[2,45,128,96]{2,0,1,3:T(2,128)(2,1)S(1)}, u32[]{:S(2)}, u32[]{:S(2)}) %all-to-all-start.2) | async-done | bytes 2211872 | tf_op jit(solution)/shard_map/all_to_all | solution.py:86
  195.5 8.2 %copy.87 = bf16[2,45,512,24]{1,3,0,2:T(8,128)(2,1)} copy(bf16[2,45,512,24]{2,3,0,1:T(8,128)(2,1)S(1)} %fusion.26) | data formatting | bytes 4423680 | tf_op jit(solution)/shard_map/convert_element_type | solution.py:89
  203.7 13.5 %reshape.178 = bf16[4,2,138240]{2,1,0:T(2,128)(2,1)} reshape(bf16[512,2,24,45]{3,2,1,0:T(8,128)(2,1)} %bitcast.156) | data formatting | bytes 4423680
  221.8 26.3 %all-to-all-done.3 = bf16[4,2,138240]{2,1,0:T(2,128)(2,1)S(1)} async-done(((bf16[4,2,138240]{2,1,0:T(2,128)(2,1)}), bf16[4,2,138240]{2,1,0:T(2,128)(2,1)S(1)}, u32[]{:S(2)}, u32[]{:S(2)}) %all-to-all-start.3) | async-done | bytes 2211872 | tf_op jit(solution)/shard_map/all_to_all | solution.py:90
  248.1 19.2 %reshape.179 = bf16[512,2,24,45]{3,2,1,0:T(8,128)(2,1)} reshape(bf16[4,2,138240]{2,1,0:T(2,128)(2,1)S(1)} %all-to-all-done.3) | data formatting | bytes 4423680
  267.3 7.8 %copy.88 = bf16[2,45,4,128,24]{3,4,2,0,1:T(8,128)(2,1)S(1)} copy(bf16[2,45,4,128,24]{1,4,0,3,2:T(8,128)(2,1)} %bitcast.157) | data formatting | bytes 4423680 | tf_op jit(solution)/shard_map/all_to_all | solution.py:90
  279.9 29.8 %all_to_all.132 = bf16[2,45,128,96]{2,0,1,3:T(2,128)(2,1)S(1)} all-to-all(bf16[2,45,128,96]{2,0,1,3:T(2,128)(2,1)S(1)} %copy.90), channel_id=1, replica_groups=mesh['lat'=4,'lon'=16,'ch'=4] {'lat'}, dimensions={3} | all-to-all | bytes 4423680 | tf_op jit(solution)/shard_map/all_to_all | solution.py:86
  318.6 8.2 %copy.92 = bf16[2,45,512,24]{1,3,0,2:T(8,128)(2,1)} copy(bf16[2,45,512,24]{2,3,0,1:T(8,128)(2,1)S(1)} %fusion.28) | data formatting | bytes 4423680 | tf_op jit(solution)/shard_map/convert_element_type | solution.py:89
  326.8 12.6 %reshape.180 = bf16[4,2,138240]{2,1,0:T(2,128)(2,1)S(1)} reshape(bf16[512,2,24,45]{3,2,1,0:T(8,128)(2,1)} %bitcast.158) | data formatting | bytes 4423680
  339.5 30.3 %all_to_all.133 = bf16[4,2,138240]{2,1,0:T(2,128)(2,1)} all-to-all(bf16[4,2,138240]{2,1,0:T(2,128)(2,1)S(1)} %reshape.180), channel_id=1, replica_groups=mesh['lat'=4,'lon'=16,'ch'=4] {'lat'}, dimensions={0} | all-to-all | bytes 4423680 | tf_op jit(solution)/shard_map/all_to_all | solution.py:90
  369.8 20.1 %reshape.181 = bf16[512,2,24,45]{3,2,1,0:T(8,128)(2,1)} reshape(bf16[4,2,138240]{2,1,0:T(2,128)(2,1)} %all_to_all.133) | data formatting | bytes 4423680
  393.8 52.8 %copy.122 = bf16[2,45,12288]{1,0,2:T(2,128)(2,1)} copy(bf16[2,45,12288]{1,2,0:T(8,128)(2,1)S(1)} %bitcast.154) | data formatting | bytes 4423680 | tf_op jit(solution)/shard_map/reshape | solution.py:119
  446.5 12.6 %reshape.182 = bf16[16,2,34560]{2,1,0:T(2,128)(2,1)} reshape(bf16[12288,2,45]{2,1,0:T(2,128)(2,1)} %bitcast.155) | data formatting | bytes 4423680
  463.8 7.7 %slice_multiply_fusion = (f32[1440,720]{1,0:T(8,128)}, f32[1440,720]{1,0:T(8,128)}) fusion(f32[1440,1440]{1,0:T(8,128)} %copy-done.1, f32[720]{0:T(1024)S(1)} %fusion.69, f32[1440,1440]{1,0:T(8,128)} %copy-done), kind=kLoop, calls=%fused_computation.18 | loop fusion | flops 3110400 | bytes 16591680 | tf_op jit(solution)/shard_map/mul | solution.py:25
  471.5 45.1 %all-to-all-done.6 = bf16[16,2,34560]{2,1,0:T(2,128)(2,1)S(1)} async-done(((bf16[16,2,34560]{2,1,0:T(2,128)(2,1)}), bf16[16,2,34560]{2,1,0:T(2,128)(2,1)S(1)}, u32[]{:S(2)}, u32[]{:S(2)}) %all-to-all-start.6) | async-done | bytes 2211872 | tf_op jit(solution)/shard_map/all_to_all | solution.py:120
  516.6 18.6 %reshape.183 = bf16[12288,2,45]{2,1,0:T(2,128)(2,1)} reshape(bf16[16,2,34560]{2,1,0:T(2,128)(2,1)S(1)} %all-to-all-done.6) | data formatting | bytes 4423680
  535.2 14.6 %copy.107 = bf16[2,45,16,768]{3,1,2,0:T(8,128)(2,1)S(1)} copy(bf16[2,45,16,768]{1,0,3,2:T(2,128)(2,1)} %bitcast.159) | data formatting | bytes 4423680 | tf_op jit(solution)/shard_map/all_to_all | solution.py:120
  552.0 10.0 %add_convert_fusion = bf16[1440,768]{1,0:T(8,128)(2,1)} fusion(bf16[1440,768]{1,0:T(8,128)(2,1)} %all_to_all.99, bf16[1440,768]{1,0:T(8,128)(2,1)} %reshape.163, f32[1440,720]{1,0:T(8,128)} %get-tuple-element.20, f32[1440,720]{1,0:T(8,128)} %get-tuple-element.19), kind=kOutput, calls=%fused_computation.26 | convolution fusion | flops 3194588160 | bytes 14929920 | tf_op jit(solution)/shard_map/dot_general | solution.py:122
  564.6 62.8 %all_to_all.134 = bf16[16,90,768]{2,1,0:T(8,128)(2,1)S(1)} all-to-all(bf16[16,90,768]{2,1,0:T(8,128)(2,1)S(1)} %all_to_all.120), channel_id=1, replica_groups=mesh['lat'=4,'lon'=16,'ch'=4] {'lon'}, dimensions={0} | all-to-all | bytes 4423680 | tf_op jit(solution)/shard_map/all_to_all | solution.py:125
  (54 shorter events, 89.5 us)
Async XLA Ops:
  4.5 66.6 %all-to-all-start = ((bf16[90,16,768]{2,0,1:T(8,128)(2,1)}), bf16[90,16,768]{2,0,1:T(8,128)(2,1)S(1)}, u32[]{:S(2)}, u32[]{:S(2)}) async-start(bf16[90,16,768]{2,0,1:T(8,128)(2,1)} %copy.81), calls=%async_computation | async-start | bytes 4718592 | tf_op jit(solution)/shard_map/all_to_all | solution.py:109
  52.6 3.4 copy-start.1
  52.6 7.3 %copy-start = (f32[1440,1440]{1,0:T(8,128)}, f32[1440,1440]{1,0:T(8,128)S(1)}, u32[]{:S(2)}) copy-start(f32[1440,1440]{1,0:T(8,128)S(1)} %get-tuple-element.23) | copy-start | bytes 24883204
  155.4 30.6 %all-to-all-start.2 = ((bf16[2,45,128,96]{2,0,1,3:T(2,128)(2,1)}), bf16[2,45,128,96]{2,0,1,3:T(2,128)(2,1)S(1)}, u32[]{:S(2)}, u32[]{:S(2)}) async-start(bf16[2,45,128,96]{2,0,1,3:T(2,128)(2,1)} %copy.84), calls=%async_computation.2 | async-start | bytes 4423680 | tf_op jit(solution)/shard_map/all_to_all | solution.py:86
  217.2 4.0 copy-start.2
  217.2 4.3 copy-start.3
  217.2 30.9 %all-to-all-start.3 = ((bf16[4,2,138240]{2,1,0:T(2,128)(2,1)}), bf16[4,2,138240]{2,1,0:T(2,128)(2,1)S(1)}, u32[]{:S(2)}, u32[]{:S(2)}) async-start(bf16[4,2,138240]{2,1,0:T(2,128)(2,1)} %reshape.178), calls=%async_computation.3 | async-start | bytes 4423680 | tf_op jit(solution)/shard_map/all_to_all | solution.py:90
  267.3 7.8 %copy-start.4 = (f32[1,2,96]{2,1,0:T(2,128)S(1)}, f32[1,2,96]{2,1,0:T(2,128)}, u32[]{:S(2)}) copy-start(f32[1,2,96]{2,1,0:T(2,128)} %param.7) | copy-start | bytes 2308
  275.1 0.8 copy-start.5
  459.1 57.5 %all-to-all-start.6 = ((bf16[16,2,34560]{2,1,0:T(2,128)(2,1)}), bf16[16,2,34560]{2,1,0:T(2,128)(2,1)S(1)}, u32[]{:S(2)}, u32[]{:S(2)}) async-start(bf16[16,2,34560]{2,1,0:T(2,128)(2,1)} %reshape.182), calls=%async_computation.6 | async-start | bytes 4423680 | tf_op jit(solution)/shard_map/all_to_all | solution.py:120
where the time goes:
time: 643 us; the launch traced here: 631 us
  local copies, waits for them, and re-layouts  237 us (37%)
  blocking collectives  184 us (29%)
  waiting for transfers between devices  94.9 us (15%)
  other arithmetic  59.1 us (9%)
  matrix products  31.7 us (5%)
  starting transfers between devices  23.6 us (4%)
    unnamed x23, local copies, waits for them, and re-layouts  104 us
    all_to_all x1, blocking collectives, per_device(): lax.all_to_all(grid_out.astype(jnp.bfloat16), 'lon', split_axis=0, concat...  62.8 us
    all_to_all x1, blocking collectives, per_device(): lax.all_to_all(spectra, 'lon', split_axis=1, concat_axis=2, tiled=True)  61.5 us
    reshape x1, local copies, waits for them, and re-layouts, per_device(): returned = returned.reshape(2, returned.shape[1], local_lat * local_chan)  52.8 us
    all_to_all x1, waiting for transfers between devices, per_device(): lax.all_to_all(returned, 'lon', split_axis=2, concat_axis=1, tiled=True)  45.1 us
    sin x2, other arithmetic, phase_tables(): return (jnp.cos(angles), jnp.sin(angles))  40.9 us
    all_to_all x1, blocking collectives, lat_apply(): lax.all_to_all(result, 'lat', split_axis=2, concat_axis=3, tiled=True)  30.3 us
    all_to_all x1, blocking collectives, lat_apply(): lax.all_to_all(data, 'lat', split_axis=3, concat_axis=2, tiled=True)  29.8 us
  transfers between devices with their start and end apart: 4, of which 4 were waited for; matrix products, arithmetic and copies ran while one was open for 10% of the time, Pallas kernels for 0%

commit v1 on v0

--- a/solution.py
+++ b/solution.py
@@ -117,7 +117,10 @@
     shrunk = block_mixing(mode_data, first_weight, first_bias, second_weight, second_bias)
     returned = lat_apply(shrunk, lat_inverse)
     returned = returned.reshape(2, returned.shape[1], local_lat * local_chan)
-    returned = lax.all_to_all(returned, "lon", split_axis=2, concat_axis=1, tiled=True)
+    returned = jnp.concatenate(
+        lax.all_to_all(jnp.stack(jnp.split(returned, lax.axis_size("lon"), axis=2)), "lon", 0, 0),
+        axis=1,
+    )
     columns = returned.reshape(2 * kept_modes, returned.shape[2])
     grid_out = jnp.dot(lon_inverse, columns, preferred_element_type=jnp.float32) + gathered.astype(
         jnp.float32

time: 643 us -> 570 us (0.89)
  local copies, waits for them, and re-layouts: 237 us -> 164 us
    reshape x2 -> x1, local copies, waits for them, and re-layouts: 55 us -> 1.94 us  [per_device(): jnp.concatenate(lax.all_to_all(jnp.stack(jnp.split(returned, lax.axis_siz...]
    unnamed x23 -> x38, local copies, waits for them, and re-layouts: 104 us -> 85.5 us
    all_to_all x1 -> x0, local copies, waits for them, and re-layouts: 14.6 us -> none  [per_device(): lax.all_to_all(returned, 'lon', split_axis=2, concat_axis=1, tiled=True)]
    another operation x0 -> x3, local copies, waits for them, and re-layouts: none -> 12.7 us  [the longest x2 10.4 us: per_device(): jnp.stack(jnp.split(returned, lax.axis_size('lon'), axis=2))]
  transfers between devices with their start and end apart: 4 -> 4, of which waited for: 4 -> 4; matrix products, arithmetic and copies ran while one was open for 10% -> 11% of each run, Pallas kernels for 0% -> 0%
where the time goes in v1:
time: 570 us; the launch traced here: 558 us
  blocking collectives  184 us (32%)
  local copies, waits for them, and re-layouts  164 us (29%)
  waiting for transfers between devices  95.3 us (17%)
  other arithmetic  58.8 us (10%)
  matrix products  31.7 us (6%)
  starting transfers between devices  23.8 us (4%)
    unnamed x38, local copies, waits for them, and re-layouts  85.5 us
    all_to_all x1, blocking collectives, per_device(): lax.all_to_all(grid_out.astype(jnp.bfloat16), 'lon', split_axis=0, concat...  62.8 us
    all_to_all x1, blocking collectives, per_device(): lax.all_to_all(spectra, 'lon', split_axis=1, concat_axis=2, tiled=True)  61.5 us
    all_to_all x1, waiting for transfers between devices, per_device(): lax.all_to_all(jnp.stack(jnp.split(returned, lax.axis_size('lon'), axis=2...  45.2 us
    sin x2, other arithmetic, phase_tables(): return (jnp.cos(angles), jnp.sin(angles))  40.7 us
    all_to_all x1, blocking collectives, lat_apply(): lax.all_to_all(result, 'lat', split_axis=2, concat_axis=3, tiled=True)  30.1 us
    all_to_all x1, blocking collectives, lat_apply(): lax.all_to_all(data, 'lat', split_axis=3, concat_axis=2, tiled=True)  29.6 us
    all_to_all x1, waiting for transfers between devices, lat_apply(): lax.all_to_all(result, 'lat', split_axis=2, concat_axis=3, tiled=True)  26.3 us
  transfers between devices with their start and end apart: 4, of which 4 were waited for; matrix products, arithmetic and copies ran while one was open for 11% of the time, Pallas kernels for 0%

profile of v1, /device:TPU:38, one launch (start us, length us, event | category | flops | bytes accessed | tf_op | source)
XLA Modules:
  0.0 558.5 jit_solution(2583909220617753023)
XLA Ops:
  4.5 11.2 %all-to-all-start = ((bf16[90,16,768]{2,0,1:T(8,128)(2,1)}), bf16[90,16,768]{2,0,1:T(8,128)(2,1)S(1)}, u32[]{:S(2)}, u32[]{:S(2)}) async-start(bf16[90,16,768]{2,0,1:T(8,128)(2,1)} %copy.132), calls=%async_computation | async-start | bytes 4718592 | tf_op jit(solution)/shard_map/all_to_all | solution.py:109
  15.7 36.6 %fusion.6 = (f32[1440,1440]{1,0:T(8,128)S(1)}, f32[1440,1440]{1,0:T(8,128)S(1)}) fusion(), kind=kLoop, calls=%fused_computation.10 | loop fusion | flops 18662400 | bytes 16588800 | tf_op jit(solution)/shard_map/sin | solution.py:14
  62.2 9.0 %all-to-all-done = bf16[90,16,768]{2,0,1:T(8,128)(2,1)S(1)} async-done(((bf16[90,16,768]{2,0,1:T(8,128)(2,1)}), bf16[90,16,768]{2,0,1:T(8,128)(2,1)S(1)}, u32[]{:S(2)}, u32[]{:S(2)}) %all-to-all-start) | async-done | bytes 2211872 | tf_op jit(solution)/shard_map/all_to_all | solution.py:109
  73.2 7.8 %fusion.20 = bf16[1440,768]{1,0:T(8,128)(2,1)S(1)} fusion(bf16[1440,768]{1,0:T(8,128)(2,1)} %all_to_all.91, f32[720,1440]{1,0:T(8,128)} %slice_negate_fusion, f32[720,1440]{1,0:T(8,128)} %slice.34), kind=kOutput, calls=%fused_computation.33 | convolution fusion | flops 3192376320 | bytes 12718080 | tf_op jit(solution)/shard_map/dot_general | solution.py:110
  82.8 61.5 %all_to_all.121 = bf16[2,720,768]{2,0,1:T(2,128)(2,1)S(1)} all-to-all(bf16[2,720,768]{2,0,1:T(2,128)(2,1)S(1)} %copy.133), channel_id=1, replica_groups=mesh['lat'=4,'lon'=16,'ch'=4] {'lon'}, dimensions={1} | all-to-all | bytes 4423680 | tf_op jit(solution)/shard_map/all_to_all | solution.py:114
  145.9 5.0 reshape.157
  171.3 14.9 %all-to-all-done.2 = bf16[2,45,128,96]{2,0,1,3:T(2,128)(2,1)S(1)} async-done(((bf16[2,45,128,96]{2,0,1,3:T(2,128)(2,1)}), bf16[2,45,128,96]{2,0,1,3:T(2,128)(2,1)S(1)}, u32[]{:S(2)}, u32[]{:S(2)}) %all-to-all-start.2) | async-done | bytes 2211872 | tf_op jit(solution)/shard_map/all_to_all | solution.py:86
  190.3 5.4 fusion.26
  195.7 8.2 %copy.138 = bf16[2,45,512,24]{1,3,0,2:T(8,128)(2,1)} copy(bf16[2,45,512,24]{2,3,0,1:T(8,128)(2,1)S(1)} %fusion.26) | data formatting | bytes 4423680 | tf_op jit(solution)/shard_map/convert_element_type | solution.py:89
  203.9 13.5 %reshape.177 = bf16[4,2,138240]{2,1,0:T(2,128)(2,1)} reshape(bf16[512,2,24,45]{3,2,1,0:T(8,128)(2,1)} %bitcast.212) | data formatting | bytes 4423680
  222.0 26.3 %all-to-all-done.3 = bf16[4,2,138240]{2,1,0:T(2,128)(2,1)S(1)} async-done(((bf16[4,2,138240]{2,1,0:T(2,128)(2,1)}), bf16[4,2,138240]{2,1,0:T(2,128)(2,1)S(1)}, u32[]{:S(2)}, u32[]{:S(2)}) %all-to-all-start.3) | async-done | bytes 2211872 | tf_op jit(solution)/shard_map/all_to_all | solution.py:90
  248.2 19.3 %reshape.178 = bf16[512,2,24,45]{3,2,1,0:T(8,128)(2,1)} reshape(bf16[4,2,138240]{2,1,0:T(2,128)(2,1)S(1)} %all-to-all-done.3) | data formatting | bytes 4423680
  267.5 7.8 %copy.139 = bf16[2,45,4,128,24]{3,4,2,0,1:T(8,128)(2,1)S(1)} copy(bf16[2,45,4,128,24]{1,4,0,3,2:T(8,128)(2,1)} %bitcast.213) | data formatting | bytes 4423680 | tf_op jit(solution)/shard_map/all_to_all | solution.py:90
  280.1 29.6 %all_to_all.122 = bf16[2,45,128,96]{2,0,1,3:T(2,128)(2,1)S(1)} all-to-all(bf16[2,45,128,96]{2,0,1,3:T(2,128)(2,1)S(1)} %copy.141), channel_id=1, replica_groups=mesh['lat'=4,'lon'=16,'ch'=4] {'lat'}, dimensions={3} | all-to-all | bytes 4423680 | tf_op jit(solution)/shard_map/all_to_all | solution.py:86
  313.2 5.4 fusion.28
  318.6 8.2 %copy.143 = bf16[2,45,512,24]{1,3,0,2:T(8,128)(2,1)} copy(bf16[2,45,512,24]{2,3,0,1:T(8,128)(2,1)S(1)} %fusion.28) | data formatting | bytes 4423680 | tf_op jit(solution)/shard_map/convert_element_type | solution.py:89
  326.8 12.6 %reshape.179 = bf16[4,2,138240]{2,1,0:T(2,128)(2,1)S(1)} reshape(bf16[512,2,24,45]{3,2,1,0:T(8,128)(2,1)} %bitcast.214) | data formatting | bytes 4423680
  339.5 30.1 %all_to_all.123 = bf16[4,2,138240]{2,1,0:T(2,128)(2,1)} all-to-all(bf16[4,2,138240]{2,1,0:T(2,128)(2,1)S(1)} %reshape.179), channel_id=1, replica_groups=mesh['lat'=4,'lon'=16,'ch'=4] {'lat'}, dimensions={0} | all-to-all | bytes 4423680 | tf_op jit(solution)/shard_map/all_to_all | solution.py:90
  369.6 20.1 %reshape.180 = bf16[512,2,24,45]{3,2,1,0:T(8,128)(2,1)} reshape(bf16[4,2,138240]{2,1,0:T(2,128)(2,1)} %all_to_all.123) | data formatting | bytes 4423680
  406.1 9.7 %copy.145 = bf16[16,2,45,768]{3,1,2,0:T(2,128)(2,1)} copy(bf16[16,2,45,768]{2,3,1,0:T(8,128)(2,1)} %fusion.65) | data formatting | bytes 4423680 | tf_op jit(solution)/shard_map/stack | solution.py:121
  420.4 7.7 %slice_multiply_fusion = (f32[1440,720]{1,0:T(8,128)}, f32[1440,720]{1,0:T(8,128)}) fusion(f32[1440,1440]{1,0:T(8,128)} %copy-done.1, f32[720]{0:T(1024)S(1)} %fusion.85, f32[1440,1440]{1,0:T(8,128)} %copy-done), kind=kLoop, calls=%fused_computation.18 | loop fusion | flops 3110400 | bytes 16591680 | tf_op jit(solution)/shard_map/mul | solution.py:25
  428.1 45.2 %all-to-all-done.6 = bf16[16,2,45,768]{3,1,2,0:T(2,128)(2,1)S(1)} async-done(((bf16[16,2,45,768]{3,1,2,0:T(2,128)(2,1)}), bf16[16,2,45,768]{3,1,2,0:T(2,128)(2,1)S(1)}, u32[]{:S(2)}, u32[]{:S(2)}) %all-to-all-start.6) | async-done | bytes 2211872 | tf_op jit(solution)/shard_map/all_to_all | solution.py:121
  478.8 10.0 %add_convert_fusion = bf16[1440,768]{1,0:T(8,128)(2,1)} fusion(bf16[1440,768]{1,0:T(8,128)(2,1)} %all_to_all.91, bf16[1440,768]{1,0:T(8,128)(2,1)} %reshape_reshape.3, f32[1440,720]{1,0:T(8,128)} %get-tuple-element.20, f32[1440,720]{1,0:T(8,128)} %get-tuple-element.19), kind=kOutput, calls=%fused_computation.26 | convolution fusion | flops 3194588160 | bytes 14929920 | tf_op jit(solution)/shard_map/dot_general | solution.py:125
  491.5 62.8 %all_to_all.124 = bf16[16,90,768]{2,1,0:T(8,128)(2,1)S(1)} all-to-all(bf16[16,90,768]{2,1,0:T(8,128)(2,1)S(1)} %all_to_all.110), channel_id=1, replica_groups=mesh['lat'=4,'lon'=16,'ch'=4] {'lon'}, dimensions={0} | all-to-all | bytes 4423680 | tf_op jit(solution)/shard_map/all_to_all | solution.py:128
  (70 shorter events, 89.6 us)
Async XLA Ops:
  4.5 66.6 %all-to-all-start = ((bf16[90,16,768]{2,0,1:T(8,128)(2,1)}), bf16[90,16,768]{2,0,1:T(8,128)(2,1)S(1)}, u32[]{:S(2)}, u32[]{:S(2)}) async-start(bf16[90,16,768]{2,0,1:T(8,128)(2,1)} %copy.132), calls=%async_computation | async-start | bytes 4718592 | tf_op jit(solution)/shard_map/all_to_all | solution.py:109
  52.3 3.4 copy-start.1
  52.3 7.3 %copy-start = (f32[1440,1440]{1,0:T(8,128)}, f32[1440,1440]{1,0:T(8,128)S(1)}, u32[]{:S(2)}) copy-start(f32[1440,1440]{1,0:T(8,128)S(1)} %get-tuple-element.23) | copy-start | bytes 24883204
  155.4 30.9 %all-to-all-start.2 = ((bf16[2,45,128,96]{2,0,1,3:T(2,128)(2,1)}), bf16[2,45,128,96]{2,0,1,3:T(2,128)(2,1)S(1)}, u32[]{:S(2)}, u32[]{:S(2)}) async-start(bf16[2,45,128,96]{2,0,1,3:T(2,128)(2,1)} %copy.135), calls=%async_computation.2 | async-start | bytes 4423680 | tf_op jit(solution)/shard_map/all_to_all | solution.py:86
  203.9 17.5 %copy-start.3 = (bf16[1,2,96,96]{3,2,1,0:T(8,128)(2,1)S(1)}, bf16[1,2,96,96]{3,2,1,0:T(8,128)(2,1)}, u32[]{:S(2)}) copy-start(bf16[1,2,96,96]{3,2,1,0:T(8,128)(2,1)} %param.6) | copy-start | bytes 110596
  217.4 4.2 copy-start.4
  217.4 30.8 %all-to-all-start.3 = ((bf16[4,2,138240]{2,1,0:T(2,128)(2,1)}), bf16[4,2,138240]{2,1,0:T(2,128)(2,1)S(1)}, u32[]{:S(2)}, u32[]{:S(2)}) async-start(bf16[4,2,138240]{2,1,0:T(2,128)(2,1)} %reshape.177), calls=%async_computation.3 | async-start | bytes 4423680 | tf_op jit(solution)/shard_map/all_to_all | solution.py:90
  267.5 7.8 %copy-start.5 = (f32[1,2,96]{2,1,0:T(2,128)S(1)}, f32[1,2,96]{2,1,0:T(2,128)}, u32[]{:S(2)}) copy-start(f32[1,2,96]{2,1,0:T(2,128)} %param.7) | copy-start | bytes 2308
  267.5 8.6 %copy-start.6 = (f32[1,2,96]{2,1,0:T(2,128)S(1)}, f32[1,2,96]{2,1,0:T(2,128)}, u32[]{:S(2)}) copy-start(f32[1,2,96]{2,1,0:T(2,128)} %param.9) | copy-start | bytes 2308
  415.8 57.5 %all-to-all-start.6 = ((bf16[16,2,45,768]{3,1,2,0:T(2,128)(2,1)}), bf16[16,2,45,768]{3,1,2,0:T(2,128)(2,1)S(1)}, u32[]{:S(2)}, u32[]{:S(2)}) async-start(bf16[16,2,45,768]{3,1,2,0:T(2,128)(2,1)} %copy.145), calls=%async_computation.6 | async-start | bytes 4423680 | tf_op jit(solution)/shard_map/all_to_all | solution.py:121
  473.3 1.4 copy-start.2
